TPU v7x, 512 devices: a whole 4x4x16 slice. The times are simulated.
512 devices in a mesh: segment: 8 (over z_lo), seq: 16 (over z_hi, y, core), head: 4 (over x).
Axes of the slice: x: 4, y: 4, z: 16 (z_hi: 2, z_lo: 8; z = z_hi * 8 + z_lo), core: 2. Of those that a mesh axis runs over, the one named last changes fastest.
Arguments:
- tokens: bfloat16 [8, 4096, 1536], P('segment', ('seq', 'head'))
- lengths: int32 [8], replicated, may hold values from 2048 to 4096, as said below
- modulation: bfloat16 [8, 2, 1536], P('segment'), may hold values from -0.5 to 0.5
- gate_gain: bfloat16 [8, 1536], P('segment'), may hold values from 1 to 3
- w_qkv: bfloat16 [8, 1536, 3, 1536], P('segment', None, None, 'head')
- w_out: bfloat16 [8, 1536, 1536], P('segment', 'head'), may hold values from -0.15625 to 0.15625
Outputs:
- states: bfloat16 [8, 4096, 1536], P('segment', ('seq', 'head'))
Inputs may be any that keep to these rules, and one draw needn't show every extreme that they name: Micro-batch m has lengths[m] real tokens at the start of its 4096 slots; some micro-batch fills all 4096.
All inputs are finite; a program needn't handle non-finite values.
Results may differ from a plain program's by a relative error of at most 0.02.
Values may be sent and summed in bfloat16 or wider, within the bound.
A program may use at most 64 MiB of HBM per device.

v0:
```python
import jax
import jax.numpy as jnp
from jax import lax
from jax.sharding import PartitionSpec as P

HEAD = 128
TICKS = 2


def from_behind(value, axis, by):
    length = lax.axis_size(axis)
    return lax.ppermute(value, axis, [(i, (i + by) % length) for i in range(length)])


def layer_norm(values):
    row_mean = jnp.mean(values, axis=-1, keepdims=True)
    centered = values - row_mean
    row_var = jnp.mean(centered * centered, axis=-1, keepdims=True)
    return centered / jnp.sqrt(row_var + 1e-06)


def block_size(key_count, shard_rows):
    for candidate in (1024, 512):
        return candidate
    if key_count <= 1024:
        return key_count
    return shard_rows


def attend_block(running, query_heads, key_block, value_block, first_row, length, score_scale):
    row_max, row_sum, weighted = running
    key_count = key_block.shape[0]
    local_heads = query_heads.shape[1]
    head_size = query_heads.shape[2]
    key_heads = key_block.reshape(key_count, local_heads, head_size)
    value_heads = value_block.reshape(key_count, local_heads, head_size)
    scores = (
        jnp.einsum("rhd,khd->hrk", query_heads, key_heads, preferred_element_type=jnp.float32)
        * score_scale
    )
    key_valid = first_row + jnp.arange(key_count, dtype=jnp.int32) < length
    scores = jnp.where(key_valid[None, None, :], scores, -1e30)
    new_max = jnp.maximum(row_max, jnp.max(scores, axis=2))
    exponent = jnp.where(key_valid[None, None, :], jnp.exp(scores - new_max[:, :, None]), 0.0)
    rescale = jnp.exp(row_max - new_max)
    row_sum = row_sum * rescale + jnp.sum(exponent, axis=2)
    weighted = weighted * rescale[:, :, None] + jnp.einsum(
        "hrk,khd->hrd",
        exponent.astype(jnp.bfloat16),
        value_heads,
        preferred_element_type=jnp.float32,
    )
    return (new_max, row_sum, weighted)


def attend_piece(running, pieces, query_heads, length, score_scale, shard_rows):
    key_piece, value_piece = pieces
    key_count = key_piece.shape[0]
    block = block_size(key_count, shard_rows)
    blocks = key_count // block
    key_stack = key_piece.reshape(blocks, block, key_piece.shape[1])
    value_stack = value_piece.reshape(blocks, block, value_piece.shape[1])

    def step_block(state_now, inputs):
        key_block, value_block, block_index = inputs
        return (
            attend_block(
                state_now,
                query_heads,
                key_block,
                value_block,
                block_index * block,
                length,
                score_scale,
            ),
            None,
        )

    final, unused = lax.scan(
        step_block, running, (key_stack, value_stack, jnp.arange(blocks, dtype=jnp.int32))
    )
    return final


def per_device(tokens, lengths, modulation, gate_gain, w_qkv, w_out):
    segment_count = lax.axis_size("segment")
    position = lax.axis_index("segment")
    state = tokens[0]
    shift_scale = modulation[0].astype(jnp.float32)
    gate_row = gate_gain[0].astype(jnp.float32)
    model_width = w_qkv.shape[1]
    local_width = w_qkv.shape[3]
    local_heads = local_width // HEAD
    flat_qkv = w_qkv[0].reshape(model_width, 3 * local_width)
    out_heads = w_out[0].reshape(local_heads, HEAD, model_width)
    score_scale = HEAD ** (-0.5)
    for tick_index in range(TICKS):
        micro_index = (position - tick_index) % segment_count
        length = lax.dynamic_index_in_dim(lengths, micro_index, 0, keepdims=False)
        values = state.astype(jnp.float32)
        normed = (layer_norm(values) * (1.0 + shift_scale[1]) + shift_scale[0]).astype(jnp.bfloat16)
        projected = jnp.dot(
            lax.all_gather(normed, "head", axis=0, tiled=True),
            flat_qkv,
            preferred_element_type=jnp.float32,
        ).astype(jnp.bfloat16)
        query_rows = projected.shape[0]
        query_heads = projected[:, :local_width].reshape(query_rows, local_heads, HEAD)
        key_part = projected[:, local_width : 2 * local_width]
        value_part = projected[:, 2 * local_width :]
        initial = (
            jnp.full((local_heads, query_rows), -1e30, jnp.float32),
            jnp.zeros((local_heads, query_rows), jnp.float32),
            jnp.zeros((local_heads, query_rows, HEAD), jnp.float32),
        )
        running = attend_piece(
            initial,
            (
                lax.all_gather(key_part, "seq", axis=0, tiled=True),
                lax.all_gather(value_part, "seq", axis=0, tiled=True),
            ),
            query_heads,
            length,
            score_scale,
            query_rows,
        )
        attended = (running[2] / running[1][:, :, None]).astype(jnp.bfloat16)
        branch = lax.psum_scatter(
            jnp.einsum(
                "hrd,hdn->rn", attended, out_heads, preferred_element_type=jnp.float32
            ).astype(jnp.bfloat16),
            "head",
            scatter_dimension=0,
            tiled=True,
        ).astype(jnp.float32)
        updated = (values + gate_row * branch).astype(jnp.bfloat16)
        state = from_behind(updated, "segment", 1)
    return state[None]


def solution(mesh):
    return jax.shard_map(
        per_device,
        mesh=mesh,
        in_specs=(
            P("segment", ("seq", "head"), None),
            P(),
            P("segment", None, None),
            P("segment", None),
            P("segment", None, None, "head"),
            P("segment", "head", None),
        ),
        out_specs=P("segment", ("seq", "head"), None),
        check_vma=False,
    )
```

profile of v0, /device:TPU:8, one launch (start us, length us, event | category | flops | bytes accessed | tf_op | source)
XLA Modules:
  0.0 673.3 jit_solution(7717919724192401937)
XLA Ops:
  10.7 13.7 %all_gather.18 = bf16[256,1536]{1,0:T(8,128)(2,1)S(1)} all-gather(bf16[64,1536]{1,0:T(8,128)(2,1)S(1)} %fusion.45), channel_id=1, replica_groups=mesh['segment'=8,'seq'=16,'head'=4] {'head'}, dimensions={0}, use_global_device_ids=true | all-gather | bytes 983040 | tf_op jit(solution)/shard_map/all_gather | solution.py:103
  24.4 6.1 copy.17
  37.0 108.7 %all-gather.5.cloned.1.call-done = bf16[4096,384]{1,0:T(8,128)(2,1)} async-done(((bf16[256,384]{1,0:T(8,128)(2,1)}), bf16[4096,384]{1,0:T(8,128)(2,1)}) %all-gather.5.cloned.1.call-update) | async-done | bytes 3145744 | tf_op jit(solution)/shard_map/all_gather | solution.py:119
  145.6 101.3 %all-gather.7.cloned.1.call-done = bf16[4096,384]{1,0:T(8,128)(2,1)} async-done(((bf16[256,384]{1,0:T(8,128)(2,1)}), bf16[4096,384]{1,0:T(8,128)(2,1)}) %all-gather.7.cloned.1.call-update) | async-done | bytes 3145744 | tf_op jit(solution)/shard_map/all_gather | solution.py:120
  246.9 56.6 %while.30 = (s32[]{:T(128)}, f32[3,256]{1,0:T(4,128)S(1)}, f32[3,256]{1,0:T(4,128)S(1)}, f32[3,256,128]{2,1,0:T(8,128)}, s32[4]{0:T(128)S(1)}, /*index=5*/s32[]{...) while((s32[]{:T(128)}, f32[3,256]{1,0:T(4,128)S(1)}, ...), condition=%wide.region_5.6_spmd.clone, body=%wide.region_2.5_spmd.clone.sunk | while | flops 413177600 | bytes 21483740 | solution.py:79
  250.6 3.4 bitcast_reduce_fusion.4
  256.9 3.4 fusion.86
  264.7 3.4 bitcast_reduce_fusion.4
  278.9 3.4 bitcast_reduce_fusion.4
  293.0 3.4 bitcast_reduce_fusion.4
  306.2 21.7 %reduce-scatter.3.cloned.1.call-done = bf16[64,1536]{1,0:T(8,128)(2,1)} async-done(((bf16[256,1536]{1,0:T(8,128)(2,1)}), bf16[64,1536]{1,0:T(8,128)(2,1)}) %reduce-scatter.3.cloned.1.call-update) | async-done | bytes 196624 | tf_op jit(solution)/shard_map/reduce_scatter | solution.py:128
  329.0 3.5 collective-permute-start
  332.4 11.0 %collective-permute-done = bf16[64,1536]{1,0:T(8,128)(2,1)S(1)} collective-permute-done((bf16[64,1536]{1,0:T(8,128)(2,1)S(1)}, bf16[64,1536]{1,0:T(8,128)(2,1)S(1)}, u32[]{:S(2)}, u32[]{:S(2)}) %collective-permute-start) | collective-permute-done | bytes 196640 | tf_op jit(solution)/shard_map/ppermute | solution.py:12
  344.2 13.6 %all_gather.21 = bf16[256,1536]{1,0:T(8,128)(2,1)S(1)} all-gather(bf16[64,1536]{1,0:T(8,128)(2,1)S(1)} %fusion.41), channel_id=1, replica_groups=mesh['segment'=8,'seq'=16,'head'=4] {'head'}, dimensions={0}, use_global_device_ids=true | all-gather | bytes 983040 | tf_op jit(solution)/shard_map/all_gather | solution.py:103
  363.6 104.3 %all-gather.11.cloned.1.call-done = bf16[4096,384]{1,0:T(8,128)(2,1)} async-done(((bf16[256,384]{1,0:T(8,128)(2,1)}), bf16[4096,384]{1,0:T(8,128)(2,1)}) %all-gather.11.cloned.1.call-update) | async-done | bytes 3145744 | tf_op jit(solution)/shard_map/all_gather | solution.py:120
  467.9 101.2 %all-gather.9.cloned.1.call-done = bf16[4096,384]{1,0:T(8,128)(2,1)} async-done(((bf16[256,384]{1,0:T(8,128)(2,1)}), bf16[4096,384]{1,0:T(8,128)(2,1)}) %all-gather.9.cloned.1.call-update) | async-done | bytes 3145744 | tf_op jit(solution)/shard_map/all_gather | solution.py:119
  569.1 56.8 %while.31 = (s32[]{:T(128)}, f32[3,256]{1,0:T(4,128)S(1)}, f32[3,256]{1,0:T(4,128)S(1)}, f32[3,256,128]{2,1,0:T(8,128)}, s32[4]{0:T(128)S(1)}, /*index=5*/s32[]{...) while((s32[]{:T(128)}, f32[3,256]{1,0:T(4,128)S(1)}, ...), condition=%wide.region_12.13_spmd.clone, body=%wide.region_9.12_spmd.clone.sunk | while | flops 413177600 | bytes 21483740 | solution.py:79
  572.8 3.5 bitcast_reduce_fusion.5
  587.0 3.5 bitcast_reduce_fusion.5
  601.2 3.5 bitcast_reduce_fusion.5
  615.4 3.5 bitcast_reduce_fusion.5
  628.5 21.8 %reduce-scatter.5.cloned.1.call-done = bf16[64,1536]{1,0:T(8,128)(2,1)} async-done(((bf16[256,1536]{1,0:T(8,128)(2,1)}), bf16[64,1536]{1,0:T(8,128)(2,1)}) %reduce-scatter.5.cloned.1.call-update) | async-done | bytes 196624 | tf_op jit(solution)/shard_map/reduce_scatter | solution.py:128
  651.3 3.5 collective-permute-start.1
  654.8 11.0 %collective-permute-done.1 = bf16[64,1536]{1,0:T(8,128)(2,1)S(1)} collective-permute-done((bf16[64,1536]{1,0:T(8,128)(2,1)S(1)}, bf16[64,1536]{1,0:T(8,128)(2,1)S(1)}, u32[]{:S(2)}, u32[]{:S(2)}) %collective-permute-start.1) | collective-permute-done | bytes 196640 | tf_op jit(solution)/shard_map/ppermute | solution.py:12
  (182 shorter events, 101.6 us)
Async XLA Ops:
  6.5 297.0 %copy-start = (bf16[1,384,1536]{2,1,0:T(8,128)(2,1)S(1)}, bf16[1,384,1536]{2,1,0:T(8,128)(2,1)}, u32[]{:S(2)}) copy-start(bf16[1,384,1536]{2,1,0:T(8,128)(2,1)} %param.15) | copy-start | bytes 3538948
  6.5 139.1 %all-gather.5.cloned.1.call-start = ((), (), s32[]{:S(2)}) async-start(), calls=%async_computation.2 | async-start | bytes 3342336 | tf_op jit(solution)/shard_map/all_gather | solution.py:119
  7.4 3.3 copy-start.8
  30.5 5.9 copy-start.11
  34.5 212.4 %all-gather.7.cloned.1.call-start = ((), (), s32[]{:S(2)}) async-start(), calls=%async_computation.3 | async-start | bytes 3342336 | tf_op jit(solution)/shard_map/all_gather | solution.py:120
  35.3 292.7 %reduce-scatter.3.cloned.1.call-start = ((), (), s32[]{:S(2)}) async-start(), calls=%async_computation.4 | async-start | bytes 983040 | tf_op jit(solution)/shard_map/reduce_scatter | solution.py:128
  254.0 2.8 copy-start.12
  268.2 2.8 copy-start.12
  282.3 2.8 copy-start.12
  296.5 2.8 copy-start.12
  303.5 24.4 %copy-start.1 = (bf16[1,64,1536]{2,1,0:T(8,128)(2,1)S(1)}, bf16[1,64,1536]{2,1,0:T(8,128)(2,1)}, u32[]{:S(2)}) copy-start(bf16[1,64,1536]{2,1,0:T(8,128)(2,1)} %param.10) | copy-start | bytes 589828
  303.5 40.5 %copy-start.7 = (f32[1536]{0:T(1024)S(1)}, f32[1536]{0:T(1024)}, u32[]{:S(2)}) copy-start(f32[1536]{0:T(1024)} %copy-done.6) | copy-start | bytes 18436
  303.5 40.5 %copy-start.9 = (f32[1536]{0:T(1024)S(1)}, f32[1536]{0:T(1024)}, u32[]{:S(2)}) copy-start(f32[1536]{0:T(1024)} %copy-done.8) | copy-start | bytes 18436
  306.1 161.8 %all-gather.11.cloned.1.call-start = ((), (), s32[]{:S(2)}) async-start(), calls=%async_computation.6 | async-start | bytes 3342336 | tf_op jit(solution)/shard_map/all_gather | solution.py:120
  306.2 54.9 %copy-start.4 = (f32[1536]{0:T(1024)}, f32[1536]{0:T(1024)S(1)}, u32[]{:S(2)}) copy-start(f32[1536]{0:T(1024)S(1)} %convert_reduce_fusion.2) | copy-start | bytes 18436
  329.0 14.4 %collective-permute-start = (bf16[64,1536]{1,0:T(8,128)(2,1)S(1)}, bf16[64,1536]{1,0:T(8,128)(2,1)S(1)}, u32[]{:S(2)}, u32[]{:S(2)}) collective-permute-start(bf16[64,1536]{1,0:T(8,128)(2,1)S(1)} %fusion.46), channel_id=1, source_target_pairs={{0,64},{64,128},{128,192},{192,256},{256,320},{320,384},{384,448},... | collective-permute-start | bytes 589832 | tf_op jit(solution)/shard_map/ppermute | solution.py:12
  362.0 207.1 %all-gather.9.cloned.1.call-start = ((), (), s32[]{:S(2)}) async-start(), calls=%async_computation.5 | async-start | bytes 3342336 | tf_op jit(solution)/shard_map/all_gather | solution.py:119
  362.6 287.7 %reduce-scatter.5.cloned.1.call-start = ((), (), s32[]{:S(2)}) async-start(), calls=%async_computation.7 | async-start | bytes 983040 | tf_op jit(solution)/shard_map/reduce_scatter | solution.py:128
  576.3 2.8 copy-start.14
  590.5 2.8 copy-start.14
  604.7 2.8 copy-start.14
  625.9 24.4 %copy-start.3 = (bf16[64,1536]{1,0:T(8,128)(2,1)S(1)}, bf16[64,1536]{1,0:T(8,128)(2,1)}, u32[]{:S(2)}) copy-start(bf16[64,1536]{1,0:T(8,128)(2,1)} %copy-done.2) | copy-start | bytes 589828
  625.9 24.4 %copy-start.5 = (f32[1536]{0:T(1024)S(1)}, f32[1536]{0:T(1024)}, u32[]{:S(2)}) copy-start(f32[1536]{0:T(1024)} %copy-done.4) | copy-start | bytes 18436
  651.3 14.5 %collective-permute-start.1 = (bf16[64,1536]{1,0:T(8,128)(2,1)S(1)}, bf16[64,1536]{1,0:T(8,128)(2,1)S(1)}, u32[]{:S(2)}, u32[]{:S(2)}) collective-permute-start(bf16[64,1536]{1,0:T(8,128)(2,1)S(1)} %fusion.47), channel_id=1, source_target_pairs={{0,64},{64,128},{128,192},{192,256},{256,320},{320,384},{384,448},... | collective-permute-start | bytes 589832 | tf_op jit(solution)/shard_map/ppermute | solution.py:12
  (12 other events, 14.6 us)
Sparse Core Ops, SparseCore 0:
  34.7 110.9 all-gather.4
  148.9 97.9 all-gather.6
  306.3 21.6 reduce-scatter.2
  362.1 105.7 all-gather.10
  471.1 97.9 all-gather.8
  628.6 21.6 reduce-scatter.4
where the time goes:
time: 674 us; the launch traced here: 673 us
  waiting for transfers between devices  482 us (72%)
  matrix products  66.5 us (10%)
  local copies, waits for them, and re-layouts  39 us (6%)
  other arithmetic  31.6 us (5%)
  blocking collectives  27.3 us (4%)
  between operations  13.7 us (2%)
  starting transfers between devices  7.13 us (1%)
    all_gather x2, waiting for transfers between devices, per_device(): lax.all_gather(key_part, 'seq', axis=0, tiled=True)  210 us
    all_gather x2, waiting for transfers between devices, per_device(): lax.all_gather(value_part, 'seq', axis=0, tiled=True)  206 us
    reduce_scatter x2, waiting for transfers between devices, per_device(): lax.psum_scatter(jnp.einsum('hrd,hdn->rn', attended, out_heads, preferred...  43.5 us
    dot_general x8, matrix products, attend_block(): jnp.einsum('rhd,khd->hrk', query_heads, key_heads, preferred_element_type...  27.6 us
    dot_general x8, matrix products, attend_block(): jnp.einsum('hrk,khd->hrd', exponent.astype(jnp.bfloat16), value_heads, pr...  27.4 us
    all_gather x2, blocking collectives, per_device(): lax.all_gather(normed, 'head', axis=0, tiled=True)  27.3 us
    ppermute x2, waiting for transfers between devices, from_behind(): lax.ppermute(value, axis, [(i, (i + by) % length) for i in range(length)])  22 us
    dynamic_slice x32, local copies, waits for them, and re-layouts, attend_piece(): lax.scan(step_block, running, (key_stack, value_stack, jnp.arange(blocks,...  21.7 us
  transfers between devices with their start and end apart: 8, of which 8 were waited for; matrix products, arithmetic and copies ran while one was open for 0% of the time, Pallas kernels for 0%

commit v1 on v0

--- a/solution.py
+++ b/solution.py
@@ -117,7 +117,10 @@
             initial,
             (
                 lax.all_gather(key_part, "seq", axis=0, tiled=True),
-                lax.all_gather(value_part, "seq", axis=0, tiled=True),
+                jnp.concatenate(
+                    lax.all_to_all(jnp.stack([value_part] * lax.axis_size("seq")), "seq", 0, 0),
+                    axis=0,
+                ),
             ),
             query_heads,
             length,

time: 674 us -> 704 us (1.045)
  starting transfers between devices: 7.13 us -> 40.1 us
    all_gather x2 -> x0, waiting for transfers between devices: 206 us -> none  [per_device(): lax.all_gather(value_part, 'seq', axis=0, tiled=True)]
    all_gather x2, waiting for transfers between devices: 210 us -> 388 us  [per_device(): lax.all_gather(key_part, 'seq', axis=0, tiled=True)]
    all_to_all x0 -> x2, starting transfers between devices: none -> 32.9 us  [per_device(): lax.all_to_all(jnp.stack([value_part] * lax.axis_size('seq')), 'seq', 0, 0)]
    reduce_scatter x2, waiting for transfers between devices: 43.5 us -> 63.7 us  [per_device(): lax.psum_scatter(jnp.einsum('hrd,hdn->rn', attended, out_heads, preferred...]
  transfers between devices with their start and end apart: 8 -> 8, of which waited for: 8 -> 6; matrix products, arithmetic and copies ran while one was open for 0% -> 0% of each run, Pallas kernels for 0% -> 0%
where the time goes in v1:
time: 704 us; the launch traced here: 703 us
  waiting for transfers between devices  475 us (67%)
  matrix products  66.5 us (9%)
  local copies, waits for them, and re-layouts  43.1 us (6%)
  starting transfers between devices  40.1 us (6%)
  other arithmetic  31.6 us (4%)
  blocking collectives  27.4 us (4%)
  between operations  13.4 us (2%)
    all_gather x2, waiting for transfers between devices, per_device(): lax.all_gather(key_part, 'seq', axis=0, tiled=True)  388 us
    reduce_scatter x2, waiting for transfers between devices, per_device(): lax.psum_scatter(jnp.einsum('hrd,hdn->rn', attended, out_heads, preferred...  63.7 us
    all_to_all x2, starting transfers between devices, per_device(): lax.all_to_all(jnp.stack([value_part] * lax.axis_size('seq')), 'seq', 0, 0)  32.9 us
    dot_general x8, matrix products, attend_block(): jnp.einsum('rhd,khd->hrk', query_heads, key_heads, preferred_element_type...  27.5 us
    dot_general x8, matrix products, attend_block(): jnp.einsum('hrk,khd->hrd', exponent.astype(jnp.bfloat16), value_heads, pr...  27.4 us
    all_gather x2, blocking collectives, per_device(): lax.all_gather(normed, 'head', axis=0, tiled=True)  27.4 us
    ppermute x2, waiting for transfers between devices, from_behind(): lax.ppermute(value, axis, [(i, (i + by) % length) for i in range(length)])  22 us
    dynamic_slice x32, local copies, waits for them, and re-layouts, attend_piece(): lax.scan(step_block, running, (key_stack, value_stack, jnp.arange(blocks,...  21.7 us
  transfers between devices with their start and end apart: 8, of which 6 were waited for; matrix products, arithmetic and copies ran while one was open for 0% of the time, Pallas kernels for 0%

profile of v1, /device:TPU:8, one launch (start us, length us, event | category | flops | bytes accessed | tf_op | source)
XLA Modules:
  0.0 702.8 jit_solution(2822668099891224340)
XLA Ops:
  10.7 13.7 %all_gather.12 = bf16[256,1536]{1,0:T(8,128)(2,1)S(1)} all-gather(bf16[64,1536]{1,0:T(8,128)(2,1)S(1)} %fusion.45), channel_id=1, replica_groups=mesh['segment'=8,'seq'=16,'head'=4] {'head'}, dimensions={0}, use_global_device_ids=true | all-gather | bytes 983040 | tf_op jit(solution)/shard_map/all_gather | solution.py:103
  24.4 6.1 copy.30
  36.5 18.3 %all-to-all-start = ((bf16[16,256,384]{2,1,0:T(8,128)(2,1)}), bf16[16,256,384]{2,1,0:T(8,128)(2,1)}, u32[]{:S(2)}, u32[]{:S(2)}) async-start(bf16[16,256,384]{2,1,0:T(8,128)(2,1)} %stack.4), calls=%async_computation | async-start | bytes 6291456 | tf_op jit(solution)/shard_map/all_to_all | solution.py:121
  57.3 205.8 %all-gather.3.cloned.1.call-done = bf16[4096,384]{1,0:T(8,128)(2,1)} async-done(((bf16[256,384]{1,0:T(8,128)(2,1)}), bf16[4096,384]{1,0:T(8,128)(2,1)}) %all-gather.3.cloned.1.call-update) | async-done | bytes 3145744 | tf_op jit(solution)/shard_map/all_gather | solution.py:119
  263.1 56.5 %while.30 = (s32[]{:T(128)}, f32[3,256]{1,0:T(4,128)S(1)}, f32[3,256]{1,0:T(4,128)S(1)}, f32[3,256,128]{2,1,0:T(8,128)}, s32[4]{0:T(128)S(1)}, /*index=5*/s32[]{...) while((s32[]{:T(128)}, f32[3,256]{1,0:T(4,128)S(1)}, ...), condition=%wide.region_5.6_spmd.clone, body=%wide.region_2.5_spmd.clone.sunk | while | flops 413177600 | bytes 21483740 | solution.py:79
  266.7 3.4 bitcast_reduce_fusion.4
  287.1 3.4 fusion.86
  295.0 3.4 bitcast_reduce_fusion.4
  301.2 3.4 fusion.86
  309.1 3.4 bitcast_reduce_fusion.4
  322.2 24.0 %reduce-scatter.3.cloned.1.call-done = bf16[64,1536]{1,0:T(8,128)(2,1)} async-done(((bf16[256,1536]{1,0:T(8,128)(2,1)}), bf16[64,1536]{1,0:T(8,128)(2,1)}) %reduce-scatter.3.cloned.1.call-update) | async-done | bytes 196624 | tf_op jit(solution)/shard_map/reduce_scatter | solution.py:131
  347.3 3.5 collective-permute-start
  350.7 11.0 %collective-permute-done = bf16[64,1536]{1,0:T(8,128)(2,1)S(1)} collective-permute-done((bf16[64,1536]{1,0:T(8,128)(2,1)S(1)}, bf16[64,1536]{1,0:T(8,128)(2,1)S(1)}, u32[]{:S(2)}, u32[]{:S(2)}) %collective-permute-start) | collective-permute-done | bytes 196640 | tf_op jit(solution)/shard_map/ppermute | solution.py:12
  362.6 13.7 %all_gather.14 = bf16[256,1536]{1,0:T(8,128)(2,1)S(1)} all-gather(bf16[64,1536]{1,0:T(8,128)(2,1)S(1)} %fusion.41), channel_id=1, replica_groups=mesh['segment'=8,'seq'=16,'head'=4] {'head'}, dimensions={0}, use_global_device_ids=true | all-gather | bytes 983040 | tf_op jit(solution)/shard_map/all_gather | solution.py:103
  382.3 14.5 %all-to-all-start.1 = ((bf16[16,256,384]{2,1,0:T(8,128)(2,1)}), bf16[16,256,384]{2,1,0:T(8,128)(2,1)}, u32[]{:S(2)}, u32[]{:S(2)}) async-start(bf16[16,256,384]{2,1,0:T(8,128)(2,1)} %stack.5), calls=%async_computation.2 | async-start | bytes 6291456 | tf_op jit(solution)/shard_map/all_to_all | solution.py:121
  398.8 182.4 %all-gather.5.cloned.1.call-done = bf16[4096,384]{1,0:T(8,128)(2,1)} async-done(((bf16[256,384]{1,0:T(8,128)(2,1)}), bf16[4096,384]{1,0:T(8,128)(2,1)}) %all-gather.5.cloned.1.call-update) | async-done | bytes 3145744 | tf_op jit(solution)/shard_map/all_gather | solution.py:119
  581.2 56.7 %while.31 = (s32[]{:T(128)}, f32[3,256]{1,0:T(4,128)S(1)}, f32[3,256]{1,0:T(4,128)S(1)}, f32[3,256,128]{2,1,0:T(8,128)}, s32[4]{0:T(128)S(1)}, /*index=5*/s32[]{...) while((s32[]{:T(128)}, f32[3,256]{1,0:T(4,128)S(1)}, ...), condition=%wide.region_12.13_spmd.clone, body=%wide.region_9.12_spmd.clone.sunk | while | flops 413177600 | bytes 21483740 | solution.py:79
  584.9 3.4 bitcast_reduce_fusion.5
  599.1 3.4 bitcast_reduce_fusion.5
  613.3 3.4 bitcast_reduce_fusion.5
  627.5 3.4 bitcast_reduce_fusion.5
  640.5 39.6 %reduce-scatter.5.cloned.1.call-done = bf16[64,1536]{1,0:T(8,128)(2,1)} async-done(((bf16[256,1536]{1,0:T(8,128)(2,1)}), bf16[64,1536]{1,0:T(8,128)(2,1)}) %reduce-scatter.5.cloned.1.call-update) | async-done | bytes 196624 | tf_op jit(solution)/shard_map/reduce_scatter | solution.py:131
  681.2 3.5 collective-permute-start.1
  684.6 11.0 %collective-permute-done.1 = bf16[64,1536]{1,0:T(8,128)(2,1)S(1)} collective-permute-done((bf16[64,1536]{1,0:T(8,128)(2,1)S(1)}, bf16[64,1536]{1,0:T(8,128)(2,1)S(1)}, u32[]{:S(2)}, u32[]{:S(2)}) %collective-permute-start.1) | collective-permute-done | bytes 196640 | tf_op jit(solution)/shard_map/ppermute | solution.py:12
  (182 shorter events, 105.8 us)
Async XLA Ops:
  6.5 313.0 %copy-start = (bf16[1,384,1536]{2,1,0:T(8,128)(2,1)S(1)}, bf16[1,384,1536]{2,1,0:T(8,128)(2,1)}, u32[]{:S(2)}) copy-start(bf16[1,384,1536]{2,1,0:T(8,128)(2,1)} %param.15) | copy-start | bytes 3538948
  7.4 3.3 copy-start.8
  36.5 20.1 %copy-start.11 = (s32[8]{0:T(128)S(1)}, s32[8]{0:T(128)}, u32[]{:S(2)}) copy-start(s32[8]{0:T(128)} %param.11) | copy-start | bytes 100
  36.5 226.6 %all-to-all-start = ((bf16[16,256,384]{2,1,0:T(8,128)(2,1)}), bf16[16,256,384]{2,1,0:T(8,128)(2,1)}, u32[]{:S(2)}, u32[]{:S(2)}) async-start(bf16[16,256,384]{2,1,0:T(8,128)(2,1)} %stack.4), calls=%async_computation | async-start | bytes 6291456 | tf_op jit(solution)/shard_map/all_to_all | solution.py:121
  54.8 208.3 %all-gather.3.cloned.1.call-start = ((), (), s32[]{:S(2)}) async-start(), calls=%async_computation.4 | async-start | bytes 3342336 | tf_op jit(solution)/shard_map/all_gather | solution.py:119
  55.5 290.7 %reduce-scatter.3.cloned.1.call-start = ((), (), s32[]{:S(2)}) async-start(), calls=%async_computation.5 | async-start | bytes 983040 | tf_op jit(solution)/shard_map/reduce_scatter | solution.py:131
  270.2 2.8 copy-start.12
  284.3 2.8 copy-start.12
  298.4 2.8 copy-start.12
  312.5 2.8 copy-start.12
  319.6 26.7 %copy-start.1 = (bf16[1,64,1536]{2,1,0:T(8,128)(2,1)S(1)}, bf16[1,64,1536]{2,1,0:T(8,128)(2,1)}, u32[]{:S(2)}) copy-start(bf16[1,64,1536]{2,1,0:T(8,128)(2,1)} %param.10) | copy-start | bytes 589828
  319.6 42.8 %copy-start.7 = (f32[1536]{0:T(1024)S(1)}, f32[1536]{0:T(1024)}, u32[]{:S(2)}) copy-start(f32[1536]{0:T(1024)} %copy-done.6) | copy-start | bytes 18436
  319.6 42.8 %copy-start.9 = (f32[1536]{0:T(1024)S(1)}, f32[1536]{0:T(1024)}, u32[]{:S(2)}) copy-start(f32[1536]{0:T(1024)} %copy-done.8) | copy-start | bytes 18436
  322.2 57.3 %copy-start.4 = (f32[1536]{0:T(1024)}, f32[1536]{0:T(1024)S(1)}, u32[]{:S(2)}) copy-start(f32[1536]{0:T(1024)S(1)} %convert_reduce_fusion.2) | copy-start | bytes 18436
  347.3 14.5 %collective-permute-start = (bf16[64,1536]{1,0:T(8,128)(2,1)S(1)}, bf16[64,1536]{1,0:T(8,128)(2,1)S(1)}, u32[]{:S(2)}, u32[]{:S(2)}) collective-permute-start(bf16[64,1536]{1,0:T(8,128)(2,1)S(1)} %fusion.46), channel_id=1, source_target_pairs={{0,64},{64,128},{128,192},{192,256},{256,320},{320,384},{384,448},... | collective-permute-start | bytes 589832 | tf_op jit(solution)/shard_map/ppermute | solution.py:12
  382.3 198.9 %all-to-all-start.1 = ((bf16[16,256,384]{2,1,0:T(8,128)(2,1)}), bf16[16,256,384]{2,1,0:T(8,128)(2,1)}, u32[]{:S(2)}, u32[]{:S(2)}) async-start(bf16[16,256,384]{2,1,0:T(8,128)(2,1)} %stack.5), calls=%async_computation.2 | async-start | bytes 6291456 | tf_op jit(solution)/shard_map/all_to_all | solution.py:121
  396.9 184.3 %all-gather.5.cloned.1.call-start = ((), (), s32[]{:S(2)}) async-start(), calls=%async_computation.6 | async-start | bytes 3342336 | tf_op jit(solution)/shard_map/all_gather | solution.py:119
  397.6 282.5 %reduce-scatter.5.cloned.1.call-start = ((), (), s32[]{:S(2)}) async-start(), calls=%async_computation.7 | async-start | bytes 983040 | tf_op jit(solution)/shard_map/reduce_scatter | solution.py:131
  588.4 2.8 copy-start.14
  602.6 2.8 copy-start.14
  616.7 2.8 copy-start.14
  637.9 42.2 %copy-start.3 = (bf16[64,1536]{1,0:T(8,128)(2,1)S(1)}, bf16[64,1536]{1,0:T(8,128)(2,1)}, u32[]{:S(2)}) copy-start(bf16[64,1536]{1,0:T(8,128)(2,1)} %copy-done.2) | copy-start | bytes 589828
  637.9 42.2 %copy-start.5 = (f32[1536]{0:T(1024)S(1)}, f32[1536]{0:T(1024)}, u32[]{:S(2)}) copy-start(f32[1536]{0:T(1024)} %copy-done.4) | copy-start | bytes 18436
  681.2 14.5 %collective-permute-start.1 = (bf16[64,1536]{1,0:T(8,128)(2,1)S(1)}, bf16[64,1536]{1,0:T(8,128)(2,1)S(1)}, u32[]{:S(2)}, u32[]{:S(2)}) collective-permute-start(bf16[64,1536]{1,0:T(8,128)(2,1)S(1)} %fusion.47), channel_id=1, source_target_pairs={{0,64},{64,128},{128,192},{192,256},{256,320},{320,384},{384,448},... | collective-permute-start | bytes 589832 | tf_op jit(solution)/shard_map/ppermute | solution.py:12
  (12 other events, 14.6 us)
Sparse Core Ops, SparseCore 0:
  59.0 204.0 all-gather.2
  322.3 23.9 reduce-scatter.2
  401.0 180.1 all-gather.4
  640.6 39.4 reduce-scatter.4
